TPU v7x, 32 devices: a whole 2x2x4 slice. The times are simulated.
32 devices in a mesh: groups: 2 (over y), seq: 4 (over z), head: 4 (over x, core).
Axes of the slice: x: 2, y: 2, z: 4, core: 2. Of those that a mesh axis runs over, the one named last changes fastest.
Arguments:
- tokens: bfloat16 [4096, 4096], P(('groups', 'seq')), parts along dimension 0, may hold values from -24 to 24
- proj_weight: bfloat16 [3, 4096, 2048], P(None, 'seq', 'head'), may hold values from -1 to 1
- cluster_ids: int32 [16, 4096, 1], P('head', ('groups', 'seq')), parts along dimension 1, may hold values from 0 to 255; in each aligned block of 512 rows (0 to 511, 512 to 1023, ..., all dimensions but the last counted through in order) at most 4 rows name the same one
- centroids: float32 [32, 256, 128], P(('groups', 'head'), 'seq'), parts along dimension 0, may hold values from -3 to 3
Outputs:
- context: bfloat16 [4096, 2048], P(('groups', 'seq'), 'head'), parts along dimension 0
- new_centroids: float32 [32, 256, 128], P(('groups', 'head'), 'seq'), parts along dimension 0
There are 2 independent parts, one for each index of `groups`. A program takes and returns all parts, laid end to end along the dimension named above; an argument that names none is the same for every part. Nothing has to cross between parts.
Inputs may be any that keep to these rules, and one draw needn't show every extreme that they name: `cluster_ids`: for each head, no cluster is named by more than 4 of the 512 tokens of one aligned block (one index of seq); some blocks reach 4.
All inputs are finite; a program needn't handle non-finite values.
Results may differ from a plain program's by a relative error of at most 0.018.
Values may be sent and summed in bfloat16 or wider, within the bound.
A program may use at most 64 MiB of HBM per device.

v0:
```python
import jax
import jax.numpy as jnp
from jax import lax
from jax.sharding import PartitionSpec as P

HS = 128
CLUSTERS = 256
SLOTS = 4


def local(tokens, proj_weight, cluster_ids, centroids):
    owners = lax.axis_size("seq")
    local_rows = tokens.shape[0]
    columns = proj_weight.shape[2]
    head_count = columns // HS
    owned = CLUSTERS // owners
    capacity = owners * SLOTS
    score_scale = HS ** (-0.5)
    projected = jnp.einsum(
        "td,pdc->ptc",
        tokens,
        lax.all_gather(proj_weight, "seq", axis=1, tiled=True),
        preferred_element_type=jnp.float32,
    ).astype(jnp.bfloat16)
    per_head = projected.reshape(3, local_rows, head_count, HS).transpose(2, 1, 0, 3)
    packed = per_head.reshape(head_count, local_rows, 3 * HS)
    member = cluster_ids[:, :, 0]
    labels = jnp.arange(CLUSTERS, dtype=jnp.int32)
    onehot = (member[:, :, None] == labels[None, None, :]).astype(jnp.bfloat16)
    ordinal_rows = jnp.arange(local_rows, dtype=jnp.int32)
    earlier = (ordinal_rows[None, :] < ordinal_rows[:, None]).astype(jnp.bfloat16)
    before = jnp.einsum("ts,hsc->htc", earlier, onehot, preferred_element_type=jnp.float32)
    ranking = jnp.take_along_axis(before, member[:, :, None], axis=2)[:, :, 0].astype(jnp.int32)
    placed = member * SLOTS + ranking
    head_index = jnp.arange(head_count, dtype=jnp.int32)[:, None]
    outbox = (
        jnp.zeros((head_count, CLUSTERS * SLOTS, 3 * HS), jnp.bfloat16)
        .at[head_index, placed]
        .set(packed)
    )
    outbox = outbox.reshape(head_count, owners, owned * SLOTS, 3 * HS)
    local_counts = jnp.sum(onehot, axis=1, dtype=jnp.float32)
    tallies = local_counts.astype(jnp.int32).reshape(head_count, owners, owned)
    blocks = lax.all_to_all(outbox, "seq", split_axis=1, concat_axis=1, tiled=True)
    arrived = lax.all_to_all(tallies, "seq", split_axis=1, concat_axis=1, tiled=True)
    local_heads = blocks.shape[0]
    arranged = (
        blocks.reshape(local_heads, owners, owned, SLOTS, 3 * HS)
        .transpose(0, 2, 1, 3, 4)
        .reshape(local_heads, owned, capacity, 3 * HS)
    )
    filled = jnp.arange(SLOTS, dtype=jnp.int32)[None, None, None, :] < arrived[:, :, :, None]
    filled = filled.transpose(0, 2, 1, 3).reshape(local_heads, owned, capacity)
    queries = arranged[:, :, :, :HS]
    key_block = arranged[:, :, :, HS : 2 * HS]
    value_block = arranged[:, :, :, 2 * HS :]
    scores = (
        jnp.einsum("hcqd,hckd->hcqk", queries, key_block, preferred_element_type=jnp.float32)
        * score_scale
    )
    ordinal = jnp.arange(capacity, dtype=jnp.int32)
    causal = ordinal[None, None, None, :] <= ordinal[None, None, :, None]
    itself = ordinal[None, None, None, :] == ordinal[None, None, :, None]
    allowed = filled[:, :, None, :] & causal | itself
    scores = jnp.where(allowed, scores, -1e30)
    row_max = jnp.max(scores, axis=3, keepdims=True)
    raised = jnp.exp(scores - row_max)
    weights = (raised / jnp.sum(raised, axis=3, keepdims=True)).astype(jnp.bfloat16)
    attended = jnp.einsum(
        "hcqk,hckd->hcqd", weights, value_block, preferred_element_type=jnp.float32
    ).astype(jnp.bfloat16)
    attended = (
        attended.reshape(local_heads, owned, owners, SLOTS, HS)
        .transpose(0, 2, 1, 3, 4)
        .reshape(local_heads, owners, owned * SLOTS, HS)
    )
    returned = lax.all_to_all(attended, "seq", split_axis=1, concat_axis=1, tiled=True)
    key_sums = jnp.einsum(
        "hck,hckd->hcd", filled.astype(jnp.bfloat16), key_block, preferred_element_type=jnp.float32
    )
    counts = jnp.sum(filled, axis=2).astype(jnp.float32)
    exchanged = (returned, key_sums, counts)
    returned, key_sums, counts = exchanged
    gathered = returned.reshape(head_count, CLUSTERS * SLOTS, HS)
    mine = jax.vmap(lambda table, where: table[where])(gathered, placed)
    context = mine.transpose(1, 0, 2).reshape(local_rows, head_count * HS)
    updated = 0.25 * centroids + 0.75 * key_sums / jnp.maximum(counts, 1.0)[:, :, None]
    return (context, updated)


def solution(mesh):
    return jax.shard_map(
        local,
        mesh=mesh,
        in_specs=(
            P(("groups", "seq"), None),
            P(None, "seq", "head"),
            P("head", ("groups", "seq"), None),
            P(("groups", "head"), "seq", None),
        ),
        out_specs=(P(("groups", "seq"), "head"), P(("groups", "head"), "seq", None)),
        check_vma=False,
    )
```

profile of v0, /device:TPU:0, one launch (start us, length us, event | category | flops | bytes accessed | tf_op | source)
XLA Modules:
  0.0 396.1 jit_solution(17036133081253212412)
XLA Ops:
  7.2 4.7 %copy.40 = bf16[3,1024,512]{1,2,0:T(8,128)(2,1)} copy(bf16[3,1024,512]{2,1,0:T(8,128)(2,1)} %param.5) | data formatting | bytes 6291456 | tf_op args[1]
  13.7 6.3 %all-to-all-start = ((s32[4,1,256]{2,1,0:T(1,128)}), s32[4,1,256]{2,1,0:T(1,128)S(1)}, u32[]{:S(2)}, u32[]{:S(2)}) async-start(s32[4,1,256]{2,1,0:T(1,128)} %reshape.146), calls=%async_computation | async-start | bytes 8192 | tf_op jit(solution)/shard_map/all_to_all | solution.py:45
  20.1 0.8 fusion.8
  20.9 20.6 %gather_fusion = f32[2048]{0:T(1024)S(1)} fusion(f32[4,512,256]{1,2,0:T(8,128)S(1)} %fusion.8, s32[2048]{0:T(1024)S(1)} %bitcast.67), kind=kCustom, calls=%fused_computation | custom fusion | bytes 40960 | tf_op jit(solution)/shard_map/jit(take_along_axis)/gather | solution.py:33
  41.7 191.3 %all-gather.2.cloned.1.call-done = bf16[3,4096,512]{1,2,0:T(8,128)(2,1)} async-done(((bf16[3,1024,512]{1,2,0:T(8,128)(2,1)}), bf16[3,4096,512]{1,2,0:T(8,128)(2,1)}) %all-gather.2.cloned.1.call-update) | async-done | bytes 12582928 | tf_op jit(solution)/shard_map/all_gather | solution.py:22
  233.0 10.9 %fusion.5 = bf16[3,512,512]{2,1,0:T(8,128)(2,1)S(1)} fusion(bf16[3,4096,512]{1,2,0:T(8,128)(2,1)} %all-gather.2.cloned.1.call-done, bf16[512,4096]{1,0:T(8,128)(2,1)} %param.4), kind=kOutput, calls=%fused_computation.13 | convolution fusion | flops 6443237376 | bytes 18350080 | tf_op jit(solution)/shard_map/td,pdc->ptc/dot_general | solution.py:19
  243.9 1.2 copy.41
  245.6 1.6 copy.42
  247.2 10.9 %scatter_custom_fusion = bf16[4096,384]{1,0:T(8,128)(2,1)S(1)} fusion(s32[2048]{0:T(1024)S(1)} %bitcast.82, bf16[2048,384]{1,0:T(8,128)(2,1)} %copy.42, bf16[]{:T(256)} %constant.15.clone.1), kind=kCustom, calls=%fused_computation.15 | custom fusion | bytes 3146240
  258.1 2.0 copy.43
  260.1 3.9 all-to-all-start.1
  265.6 69.3 %all-to-all-done.1 = bf16[4,4,256,384]{3,2,0,1:T(8,128)(2,1)S(1)} async-done(((bf16[4,4,256,384]{3,2,0,1:T(8,128)(2,1)}), bf16[4,4,256,384]{3,2,0,1:T(8,128)(2,1)S(1)}, u32[]{:S(2)}, u32[]{:S(2)}) %all-to-all-start.1) | async-done | bytes 3145760 | tf_op jit(solution)/shard_map/all_to_all | solution.py:44
  334.9 2.4 copy.44
  337.3 1.6 copy.45
  338.9 2.4 reshape.108
  341.4 3.5 fusion.27
  344.9 1.7 convolution_convert_fusion
  347.1 1.1 copy.48
  348.2 3.6 all-to-all-start.2
  352.2 1.6 fusion.17
  353.9 0.8 divide_add_fusion
  354.6 22.5 %all-to-all-done.2 = bf16[4,4,256,128]{3,2,0,1:T(8,128)(2,1)S(1)} async-done(((bf16[4,4,256,128]{3,2,0,1:T(8,128)(2,1)}), bf16[4,4,256,128]{3,2,0,1:T(8,128)(2,1)S(1)}, u32[]{:S(2)}, u32[]{:S(2)}) %all-to-all-start.2) | async-done | bytes 1048608 | tf_op jit(solution)/shard_map/all_to_all | solution.py:77
  377.2 11.1 %gather_fusion.1 = bf16[2048,128]{1,0:T(8,128)(2,1)S(1)} fusion(bf16[4,1024,128]{2,1,0:T(8,128)(2,1)S(1)} %bitcast.68, s32[2048]{0:T(1024)S(1)} %bitcast.66), kind=kCustom, calls=%fused_computation.1 | custom fusion | bytes 1064960 | tf_op jit(solution)/shard_map/vmap()/gather | solution.py:85
  388.4 0.9 copy.66
  (48 shorter events, 5.0 us)
Async XLA Ops:
  7.2 225.8 %all-gather.2.cloned.1.call-start = ((), (), s32[]{:S(2)}) async-start(), calls=%async_computation.3 | async-start | bytes 15728640 | tf_op jit(solution)/shard_map/all_gather | solution.py:22
  11.9 0.7 copy-start.1
  13.7 246.4 %all-to-all-start = ((s32[4,1,256]{2,1,0:T(1,128)}), s32[4,1,256]{2,1,0:T(1,128)S(1)}, u32[]{:S(2)}, u32[]{:S(2)}) async-start(s32[4,1,256]{2,1,0:T(1,128)} %reshape.146), calls=%async_computation | async-start | bytes 8192 | tf_op jit(solution)/shard_map/all_to_all | solution.py:45
  20.8 20.6 %copy-start.2 = (s32[2]{0:T(128)S(1)}, s32[2]{0:T(128)}, u32[]{:S(2)}) copy-start(s32[2]{0:T(128)} %constant.42) | copy-start | bytes 28
  20.8 20.7 %copy-start.3 = (s32[2]{0:T(128)S(1)}, s32[2]{0:T(128)}, u32[]{:S(2)}) copy-start(s32[2]{0:T(128)} %constant.45) | copy-start | bytes 28
  260.1 74.8 %all-to-all-start.1 = ((bf16[4,4,256,384]{3,2,0,1:T(8,128)(2,1)}), bf16[4,4,256,384]{3,2,0,1:T(8,128)(2,1)S(1)}, u32[]{:S(2)}, u32[]{:S(2)}) async-start(bf16[4,4,256,384]{3,2,0,1:T(8,128)(2,1)} %copy.43), calls=%async_computation.1 | async-start | bytes 6291456 | tf_op jit(solution)/shard_map/all_to_all | solution.py:44
  348.2 5.7 %copy-start = (f32[4,64,128]{2,1,0:T(8,128)S(1)}, f32[4,64,128]{2,1,0:T(8,128)}, u32[]{:S(2)}) copy-start(f32[4,64,128]{2,1,0:T(8,128)} %param.7) | copy-start | bytes 393220
  348.2 28.9 %all-to-all-start.2 = ((bf16[4,4,256,128]{3,2,0,1:T(8,128)(2,1)}), bf16[4,4,256,128]{3,2,0,1:T(8,128)(2,1)S(1)}, u32[]{:S(2)}, u32[]{:S(2)}) async-start(bf16[4,4,256,128]{3,2,0,1:T(8,128)(2,1)} %copy.48), calls=%async_computation.2 | async-start | bytes 2097152 | tf_op jit(solution)/shard_map/all_to_all | solution.py:77
Sparse Core Ops, SparseCore 0:
  12.0 220.8 all-gather.1
where the time goes:
time: 397 us; the launch traced here: 396 us
  waiting for transfers between devices  283 us (71%)
  local copies, waits for them, and re-layouts  64.1 us (16%)
  matrix products  18.5 us (5%)
  between operations  14.3 us (4%)
  starting transfers between devices  13.9 us (4%)
    all_gather x1, waiting for transfers between devices, local(): lax.all_gather(proj_weight, 'seq', axis=1, tiled=True)  191 us
    all_to_all x1, waiting for transfers between devices, local(): lax.all_to_all(outbox, 'seq', split_axis=1, concat_axis=1, tiled=True)  69.3 us
    all_to_all x1, waiting for transfers between devices, local(): lax.all_to_all(attended, 'seq', split_axis=1, concat_axis=1, tiled=True)  22.5 us
    gather x2, local copies, waits for them, and re-layouts, local(): jnp.take_along_axis(before, member[:, :, None], axis=2)[:, :, 0]  20.6 us
    unnamed x18, local copies, waits for them, and re-layouts  17.5 us
    gather x1, local copies, waits for them, and re-layouts, local(): mine = jax.vmap(lambda table, where: table[where])(gathered, placed)  11.1 us
    dot_general x1, matrix products, local(): jnp.einsum('td,pdc->ptc', tokens, lax.all_gather(proj_weight, 'seq', axis...  10.9 us
  transfers between devices with their start and end apart: 4, of which 3 were waited for; matrix products, arithmetic and copies ran while one was open for 14% of the time, Pallas kernels for 0%

commit v1 on v0

--- a/solution.py
+++ b/solution.py
@@ -8,6 +8,18 @@
 SLOTS = 4
 
 
+def ring_product(value, axis, dim, term):
+    size, index = (lax.axis_size(axis), lax.axis_index(axis))
+    left = [(i, (i - 1) % size) for i in range(size)]
+    rows = value.shape[dim]
+    carried = value
+    so_far = term(carried, index * rows)
+    for hop in range(1, size):
+        carried = lax.ppermute(carried, axis, left)
+        so_far = so_far + term(carried, (index + hop) % size * rows)
+    return so_far
+
+
 def local(tokens, proj_weight, cluster_ids, centroids):
     owners = lax.axis_size("seq")
     local_rows = tokens.shape[0]
@@ -16,11 +28,16 @@
     owned = CLUSTERS // owners
     capacity = owners * SLOTS
     score_scale = HS ** (-0.5)
-    projected = jnp.einsum(
-        "td,pdc->ptc",
-        tokens,
-        lax.all_gather(proj_weight, "seq", axis=1, tiled=True),
-        preferred_element_type=jnp.float32,
+    projected = ring_product(
+        proj_weight,
+        "seq",
+        1,
+        lambda own_block, offset: jnp.einsum(
+            "td,pdc->ptc",
+            lax.dynamic_slice_in_dim(tokens, offset, own_block.shape[1], axis=1),
+            own_block,
+            preferred_element_type=jnp.float32,
+        ),
     ).astype(jnp.bfloat16)
     per_head = projected.reshape(3, local_rows, head_count, HS).transpose(2, 1, 0, 3)
     packed = per_head.reshape(head_count, local_rows, 3 * HS)

time: 397 us -> 367 us (0.924)
  waiting for transfers between devices: 283 us -> 253 us
  between operations: 14.3 us -> 1.03 us
  starting transfers between devices: 13.9 us -> 26.1 us
    all_gather x1 -> x0, waiting for transfers between devices: 191 us -> none  [local(): lax.all_gather(proj_weight, 'seq', axis=1, tiled=True)]
    ppermute x0 -> x3, waiting for transfers between devices: none -> 164 us  [ring_product(): carried = lax.ppermute(carried, axis, left)]
    ppermute x0 -> x3, starting transfers between devices: none -> 13.8 us  [ring_product(): carried = lax.ppermute(carried, axis, left)]
    dot_general x1 -> x4, matrix products: 10.9 us -> 14.1 us  [local(): jnp.einsum('td,pdc->ptc', lax.dynamic_slice_in_dim(tokens, offset, own_bl...]
    unnamed x18 -> x24, local copies, waits for them, and re-layouts: 17.5 us -> 15.7 us
  transfers between devices with their start and end apart: 4 -> 6, of which waited for: 3 -> 5; matrix products, arithmetic and copies ran while one was open for 14% -> 16% of each run, Pallas kernels for 0% -> 0%
where the time goes in v1:
time: 367 us; the launch traced here: 366 us
  waiting for transfers between devices  253 us (69%)
  local copies, waits for them, and re-layouts  62.3 us (17%)
  starting transfers between devices  26.1 us (7%)
  matrix products  21.7 us (6%)
    ppermute x3, waiting for transfers between devices, ring_product(): carried = lax.ppermute(carried, axis, left)  164 us
    all_to_all x1, waiting for transfers between devices, local(): lax.all_to_all(outbox, 'seq', split_axis=1, concat_axis=1, tiled=True)  66.4 us
    all_to_all x1, waiting for transfers between devices, local(): lax.all_to_all(attended, 'seq', split_axis=1, concat_axis=1, tiled=True)  22.4 us
    gather x2, local copies, waits for them, and re-layouts, local(): jnp.take_along_axis(before, member[:, :, None], axis=2)[:, :, 0]  20.6 us
    unnamed x24, local copies, waits for them, and re-layouts  15.7 us
    dot_general x4, matrix products, local(): jnp.einsum('td,pdc->ptc', lax.dynamic_slice_in_dim(tokens, offset, own_bl...  14.1 us
    ppermute x3, starting transfers between devices, ring_product(): carried = lax.ppermute(carried, axis, left)  13.8 us
    gather x1, local copies, waits for them, and re-layouts, local(): mine = jax.vmap(lambda table, where: table[where])(gathered, placed)  11.1 us
  transfers between devices with their start and end apart: 6, of which 5 were waited for; matrix products, arithmetic and copies ran while one was open for 16% of the time, Pallas kernels for 0%

profile of v1, /device:TPU:0, one launch (start us, length us, event | category | flops | bytes accessed | tf_op | source)
XLA Modules:
  0.0 365.9 jit_solution(15385009154423277328)
XLA Ops:
  0.6 3.2 copy.44
  3.8 5.1 %collective-permute-start = (bf16[3,1024,512]{1,2,0:T(8,128)(2,1)S(1)}, bf16[3,1024,512]{1,2,0:T(8,128)(2,1)S(1)}, u32[]{:S(2)}, u32[]{:S(2)}) collective-permute-start(bf16[3,1024,512]{1,2,0:T(8,128)(2,1)S(1)} %copy.44), channel_id=1, source_target_pairs={{0,12},{4,0},{8,4},{12,8},{1,13},{5,1},{9,5},{13,9},{2,14},{6,2},{... | collective-permute-start | bytes 9437192 | tf_op jit(solution)/shard_map/ppermute | solution.py:18
  9.0 67.4 %collective-permute-done = bf16[3,1024,512]{1,2,0:T(8,128)(2,1)S(1)} collective-permute-done((bf16[3,1024,512]{1,2,0:T(8,128)(2,1)S(1)}, bf16[3,1024,512]{1,2,0:T(8,128)(2,1)S(1)}, u32[]{:S(2)}, u32[]{:S(2)}) %collective-permute-start) | collective-permute-done | bytes 3145760 | tf_op jit(solution)/shard_map/ppermute | solution.py:18
  76.3 4.3 %collective-permute-start.1 = (bf16[3,1024,512]{1,2,0:T(8,128)(2,1)S(1)}, bf16[3,1024,512]{1,2,0:T(8,128)(2,1)}, u32[]{:S(2)}, u32[]{:S(2)}) collective-permute-start(bf16[3,1024,512]{1,2,0:T(8,128)(2,1)S(1)} %collective-permute-done), channel_id=1, source_target_pairs={{0,12},{4,0},{8,4},{12,8},{1,13},{5,1},{9,5},{13,9},{2,14},{6,2},{... | collective-permute-start | bytes 9437192 | tf_op jit(solution)/shard_map/ppermute | solution.py:18
  80.6 66.5 %collective-permute-done.1 = bf16[3,1024,512]{1,2,0:T(8,128)(2,1)} collective-permute-done((bf16[3,1024,512]{1,2,0:T(8,128)(2,1)S(1)}, bf16[3,1024,512]{1,2,0:T(8,128)(2,1)}, u32[]{:S(2)}, u32[]{:S(2)}) %collective-permute-start.1) | collective-permute-done | bytes 3145760 | tf_op jit(solution)/shard_map/ppermute | solution.py:18
  147.1 4.4 %collective-permute-start.2 = (bf16[3,1024,512]{1,2,0:T(8,128)(2,1)}, bf16[3,1024,512]{1,2,0:T(8,128)(2,1)}, u32[]{:S(2)}, u32[]{:S(2)}) collective-permute-start(bf16[3,1024,512]{1,2,0:T(8,128)(2,1)} %collective-permute-done.1), channel_id=1, source_target_pairs={{0,12},{4,0},{8,4},{12,8},{1,13},{5,1},{9,5},{13,9},{2,14},{6,2},{... | collective-permute-start | bytes 9437192 | tf_op jit(solution)/shard_map/ppermute | solution.py:18
  152.6 3.2 all-to-all-start
  156.7 20.6 %gather_fusion = f32[2048]{0:T(1024)S(1)} fusion(f32[4,512,256]{1,2,0:T(8,128)S(1)} %fusion.3, s32[2048]{0:T(1024)S(1)} %bitcast.77), kind=kCustom, calls=%fused_computation | custom fusion | bytes 40960 | tf_op jit(solution)/shard_map/jit(take_along_axis)/gather | solution.py:50
  177.6 4.2 %fusion.13 = f32[512,3,512]{0,2,1:T(8,128)S(1)} fusion(bf16[3,1024,512]{2,1,0:T(8,128)(2,1)} %param.5, bf16[512,4096]{1,0:T(8,128)(2,1)} %param.4, s32[]{:T(128)S(6)} %select_n.50), kind=kOutput, calls=%fused_computation.23 | convolution fusion | flops 1610612736 | bytes 7340036 | tf_op jit(solution)/shard_map/td,pdc->ptc/dot_general | solution.py:35
  182.0 1.8 fusion.11
  183.8 3.8 %fusion.9 = f32[512,3,512]{0,2,1:T(8,128)S(1)} fusion(bf16[3,1024,512]{1,2,0:T(8,128)(2,1)} %collective-permute-done.1, bf16[512,4096]{1,0:T(8,128)(2,1)S(1)} %copy-done, s32[]{:T(128)S(6)} %select_n.54), kind=kOutput, calls=%fused_computation.19 | convolution fusion | flops 1610612736 | bytes 7340036 | tf_op jit(solution)/shard_map/td,pdc->ptc/dot_general | solution.py:35
  187.6 29.9 %collective-permute-done.2 = bf16[3,1024,512]{1,2,0:T(8,128)(2,1)} collective-permute-done((bf16[3,1024,512]{1,2,0:T(8,128)(2,1)}, bf16[3,1024,512]{1,2,0:T(8,128)(2,1)}, u32[]{:S(2)}, u32[]{:S(2)}) %collective-permute-start.2) | collective-permute-done | bytes 3145760 | tf_op jit(solution)/shard_map/ppermute | solution.py:18
  217.5 4.2 %add_convert_fusion = bf16[512,3,512]{0,2,1:T(8,128)(2,1)S(1)} fusion(f32[512,3,512]{0,2,1:T(8,128)S(1)} %fusion.9, f32[512,3,512]{0,2,1:T(8,128)S(1)} %fusion.13, f32[512,3,512]{0,2,1:T(8,128)S(1)} %fusion.11, bf16[3,1024,512]{1,2,0:T(8,128)(2,1)} %collective-permute-done.2, bf16[512,4096]{1,0:T(8,128)(2,1)S(1)} %copy-done, s32[]{:T(128)S(6)} %select_n.56), kind=kOutput, calls=%fused_computation.4 | convolution fusion | flops 1613758464 | bytes 15204356 | tf_op jit(solution)/shard_map/td,pdc->ptc/dot_general | solution.py:35
  225.0 11.1 %scatter_custom_fusion = bf16[4096,384]{1,0:T(8,128)(2,1)S(1)} fusion(s32[2048]{0:T(1024)S(1)} %bitcast.92, bf16[2048,384]{1,0:T(8,128)(2,1)} %copy.46, bf16[]{:T(256)} %constant.27.clone.1), kind=kCustom, calls=%fused_computation.13 | custom fusion | bytes 3146240
  236.1 2.0 copy.47
  238.1 5.6 %all-to-all-start.1 = ((bf16[4,4,256,384]{3,2,0,1:T(8,128)(2,1)}), bf16[4,4,256,384]{3,2,0,1:T(8,128)(2,1)S(1)}, u32[]{:S(2)}, u32[]{:S(2)}) async-start(bf16[4,4,256,384]{3,2,0,1:T(8,128)(2,1)} %copy.47), calls=%async_computation.1 | async-start | bytes 6291456 | tf_op jit(solution)/shard_map/all_to_all | solution.py:61
  245.3 66.4 %all-to-all-done.1 = bf16[4,4,256,384]{3,2,0,1:T(8,128)(2,1)S(1)} async-done(((bf16[4,4,256,384]{3,2,0,1:T(8,128)(2,1)}), bf16[4,4,256,384]{3,2,0,1:T(8,128)(2,1)S(1)}, u32[]{:S(2)}, u32[]{:S(2)}) %all-to-all-start.1) | async-done | bytes 3145760 | tf_op jit(solution)/shard_map/all_to_all | solution.py:61
  311.7 2.4 copy.48
  315.8 2.4 reshape.108
  318.2 3.5 fusion.37
  321.7 1.7 convolution_convert_fusion
  325.0 3.5 all-to-all-start.2
  331.4 22.4 %all-to-all-done.2 = bf16[4,4,256,128]{3,2,0,1:T(8,128)(2,1)S(1)} async-done(((bf16[4,4,256,128]{3,2,0,1:T(8,128)(2,1)}), bf16[4,4,256,128]{3,2,0,1:T(8,128)(2,1)S(1)}, u32[]{:S(2)}, u32[]{:S(2)}) %all-to-all-start.2) | async-done | bytes 1048608 | tf_op jit(solution)/shard_map/all_to_all | solution.py:94
  353.9 11.1 %gather_fusion.1 = bf16[2048,128]{1,0:T(8,128)(2,1)S(1)} fusion(bf16[4,1024,128]{2,1,0:T(8,128)(2,1)S(1)} %bitcast.78, s32[2048]{0:T(1024)S(1)} %bitcast.76), kind=kCustom, calls=%fused_computation.1 | custom fusion | bytes 1064960 | tf_op jit(solution)/shard_map/vmap()/gather | solution.py:102
  (60 shorter events, 14.0 us)
Async XLA Ops:
  0.6 150.9 %copy-start.2 = (s32[4,512,1]{1,2,0:T(1,128)S(1)}, s32[4,512,1]{1,2,0:T(1,128)}, u32[]{:S(2)}) copy-start(s32[4,512,1]{1,2,0:T(1,128)} %param.6) | copy-start | bytes 24580
  3.8 72.5 %collective-permute-start = (bf16[3,1024,512]{1,2,0:T(8,128)(2,1)S(1)}, bf16[3,1024,512]{1,2,0:T(8,128)(2,1)S(1)}, u32[]{:S(2)}, u32[]{:S(2)}) collective-permute-start(bf16[3,1024,512]{1,2,0:T(8,128)(2,1)S(1)} %copy.44), channel_id=1, source_target_pairs={{0,12},{4,0},{8,4},{12,8},{1,13},{5,1},{9,5},{13,9},{2,14},{6,2},{... | collective-permute-start | bytes 9437192 | tf_op jit(solution)/shard_map/ppermute | solution.py:18
  76.3 70.8 %copy-start.5 = (bf16[3,1024,512]{1,2,0:T(8,128)(2,1)}, bf16[3,1024,512]{1,2,0:T(8,128)(2,1)S(1)}, u32[]{:S(2)}) copy-start(bf16[3,1024,512]{1,2,0:T(8,128)(2,1)S(1)} %collective-permute-done) | copy-start | bytes 9437188
  76.3 70.8 %collective-permute-start.1 = (bf16[3,1024,512]{1,2,0:T(8,128)(2,1)S(1)}, bf16[3,1024,512]{1,2,0:T(8,128)(2,1)}, u32[]{:S(2)}, u32[]{:S(2)}) collective-permute-start(bf16[3,1024,512]{1,2,0:T(8,128)(2,1)S(1)} %collective-permute-done), channel_id=1, source_target_pairs={{0,12},{4,0},{8,4},{12,8},{1,13},{5,1},{9,5},{13,9},{2,14},{6,2},{... | collective-permute-start | bytes 9437192 | tf_op jit(solution)/shard_map/ppermute | solution.py:18
  147.1 70.4 %collective-permute-start.2 = (bf16[3,1024,512]{1,2,0:T(8,128)(2,1)}, bf16[3,1024,512]{1,2,0:T(8,128)(2,1)}, u32[]{:S(2)}, u32[]{:S(2)}) collective-permute-start(bf16[3,1024,512]{1,2,0:T(8,128)(2,1)} %collective-permute-done.1), channel_id=1, source_target_pairs={{0,12},{4,0},{8,4},{12,8},{1,13},{5,1},{9,5},{13,9},{2,14},{6,2},{... | collective-permute-start | bytes 9437192 | tf_op jit(solution)/shard_map/ppermute | solution.py:18
  152.6 85.5 %all-to-all-start = ((s32[4,1,256]{2,1,0:T(1,128)}), s32[4,1,256]{2,1,0:T(1,128)S(1)}, u32[]{:S(2)}, u32[]{:S(2)}) async-start(s32[4,1,256]{2,1,0:T(1,128)} %reshape.149), calls=%async_computation | async-start | bytes 8192 | tf_op jit(solution)/shard_map/all_to_all | solution.py:62
  156.7 20.6 %copy-start.4 = (s32[2]{0:T(128)S(1)}, s32[2]{0:T(128)}, u32[]{:S(2)}) copy-start(s32[2]{0:T(128)} %constant.74) | copy-start | bytes 28
  156.7 20.7 %copy-start.3 = (s32[2]{0:T(128)S(1)}, s32[2]{0:T(128)}, u32[]{:S(2)}) copy-start(s32[2]{0:T(128)} %constant.77) | copy-start | bytes 28
  177.6 4.3 %copy-start = (bf16[512,4096]{1,0:T(8,128)(2,1)S(1)}, bf16[512,4096]{1,0:T(8,128)(2,1)}, u32[]{:S(2)}) copy-start(bf16[512,4096]{1,0:T(8,128)(2,1)} %param.4) | copy-start | bytes 12582916
  177.6 4.4 %copy-start.6 = (bf16[3,1024,512]{1,2,0:T(8,128)(2,1)S(1)}, bf16[3,1024,512]{1,2,0:T(8,128)(2,1)}, u32[]{:S(2)}) copy-start(bf16[3,1024,512]{1,2,0:T(8,128)(2,1)} %copy-done.5) | copy-start | bytes 9437188
  238.1 73.6 %all-to-all-start.1 = ((bf16[4,4,256,384]{3,2,0,1:T(8,128)(2,1)}), bf16[4,4,256,384]{3,2,0,1:T(8,128)(2,1)S(1)}, u32[]{:S(2)}, u32[]{:S(2)}) async-start(bf16[4,4,256,384]{3,2,0,1:T(8,128)(2,1)} %copy.47), calls=%async_computation.1 | async-start | bytes 6291456 | tf_op jit(solution)/shard_map/all_to_all | solution.py:61
  324.0 6.6 %copy-start.1 = (f32[4,64,128]{2,1,0:T(8,128)S(1)}, f32[4,64,128]{2,1,0:T(8,128)}, u32[]{:S(2)}) copy-start(f32[4,64,128]{2,1,0:T(8,128)} %param.7) | copy-start | bytes 393220
  325.0 28.8 %all-to-all-start.2 = ((bf16[4,4,256,128]{3,2,0,1:T(8,128)(2,1)}), bf16[4,4,256,128]{3,2,0,1:T(8,128)(2,1)S(1)}, u32[]{:S(2)}, u32[]{:S(2)}) async-start(bf16[4,4,256,128]{3,2,0,1:T(8,128)(2,1)} %copy.52), calls=%async_computation.2 | async-start | bytes 2097152 | tf_op jit(solution)/shard_map/all_to_all | solution.py:94
